TPU v7x, 256 devices: a whole 4x4x8 slice. The times are simulated.
256 devices in a mesh: lat: 32 (over x, z), lead: 8 (over y, core).
Axes of the slice: x: 4, y: 4, z: 8, core: 2. Of those that a mesh axis runs over, the one named last changes fastest.
Arguments:
- latent: bfloat16 [32, 256, 64, 256], P('lat', None, 'lead'), may hold values from -6 to 6
- conv_weight: bfloat16 [3, 3, 256, 256], replicated, may hold values from -0.125 to 0.125
- conv_bias: float32 [256], replicated, may hold values from -4 to 4
- norm_gain: float32 [256], replicated, may hold values from 0.1 to 1.9
- w_query: bfloat16 [256, 256], replicated, may hold values from -12 to 12
- w_key: bfloat16 [256, 256], replicated, may hold values from -0.25 to 0.25
- w_value: bfloat16 [256, 256], replicated, may hold values from -0.375 to 0.375
- w_out: bfloat16 [256, 256], replicated, may hold values from -0.375 to 0.375
Outputs:
- section_out: bfloat16 [32, 256, 64, 256], P('lat', None, 'lead')
All inputs are finite; a program needn't handle non-finite values.
Results may differ from a plain program's by a relative error of at most 0.014.
Values may be sent and summed in bfloat16 or wider, within the bound.
No kernel may reach another device: no remote copies, remote signals or barrier semaphores. Data moves between devices by JAX's collectives and lax.ppermute only.
A program may use at most 128 MiB of HBM per device.

v0:
```python
import math
import jax
import jax.numpy as jnp
from jax import lax
from jax.sharding import PartitionSpec as P

HD = 32


def padded_2(block, sides, width):
    for axis, dim in sides:
        count = lax.axis_size(axis)
        forward = [(i, i + 1) for i in range(count - 1)]
        backward = [(target, source) for source, target in forward]
        low = lax.ppermute(
            lax.slice_in_dim(block, block.shape[dim] - width, None, axis=dim), axis, forward
        )
        high = lax.ppermute(lax.slice_in_dim(block, 0, width, axis=dim), axis, backward)
        block = jnp.concatenate([low, block, high], axis=dim)
    return block


def attend(query, keys, values):
    chans = query.shape[-1]
    heads = chans // HD
    q_shape = query.shape
    query = query.reshape(-1, q_shape[-2], heads, HD)
    keys = keys.reshape(-1, keys.shape[-2], heads, HD)
    values = values.reshape(-1, values.shape[-2], heads, HD)
    scores = jnp.einsum(
        "pqhd,pkhd->phqk", query, keys, preferred_element_type=jnp.float32
    ) / math.sqrt(HD)
    top = jnp.max(scores, axis=-1, keepdims=True)
    expo = jnp.exp(scores - top)
    weights = (expo / jnp.sum(expo, axis=-1, keepdims=True)).astype(jnp.bfloat16)
    attended = jnp.einsum("phqk,pkhd->pqhd", weights, values, preferred_element_type=jnp.float32)
    return attended.astype(jnp.bfloat16).reshape(q_shape)


def project(normed, weight):
    shape = normed.shape
    flat = jnp.dot(normed.reshape(-1, shape[-1]), weight, preferred_element_type=jnp.float32)
    return flat.astype(jnp.bfloat16).reshape(shape)


def shards(latent, conv_weight, conv_bias, norm_gain, w_query, w_key, w_value, w_out):
    nrows, width, leads, chans = latent.shape
    extended = padded_2(latent, (("lat", 0),), 1)
    padded = jnp.pad(extended, ((0, 0), (1, 1), (0, 0), (0, 0)))
    acc = jnp.zeros((nrows * width * leads, chans), jnp.float32)
    for a in range(3):
        for b in range(3):
            piece = padded[a : a + nrows, b : b + width].reshape(-1, chans)
            acc = acc + jnp.dot(piece, conv_weight[a, b], preferred_element_type=jnp.float32)
    hidden = jax.nn.gelu(acc + conv_bias, approximate=True).astype(jnp.bfloat16)
    hidden_f = hidden.astype(jnp.float32)
    mean = jnp.mean(hidden_f, axis=-1, keepdims=True)
    var = jnp.mean((hidden_f - mean) ** 2, axis=-1, keepdims=True)
    normed = ((hidden_f - mean) * lax.rsqrt(var + 1e-05) * norm_gain).astype(jnp.bfloat16)
    normed = normed.reshape(nrows, width, leads, chans)
    block = lax.all_to_all(normed, "lead", split_axis=1, concat_axis=2, tiled=True)
    attended_px = attend(project(block, w_query), project(block, w_key), project(block, w_value))
    attended = lax.all_to_all(attended_px, "lead", split_axis=2, concat_axis=1, tiled=True)
    mixed = hidden_f + jnp.dot(
        attended.reshape(-1, chans), w_out, preferred_element_type=jnp.float32
    )
    return mixed.astype(jnp.bfloat16).reshape(nrows, width, leads, chans)


def solution(mesh):
    in_specs = (P("lat", None, "lead", None), P(), P(), P(), P(), P(), P(), P())
    out_specs = P("lat", None, "lead", None)
    return jax.shard_map(shards, mesh=mesh, in_specs=in_specs, out_specs=out_specs, check_vma=False)
```

profile of v0, /device:TPU:6, one launch (start us, length us, event | category | flops | bytes accessed | tf_op | source)
XLA Modules:
  0.0 127.0 jit_solution(6796232368115607537)
XLA Ops:
  0.0 0.0 copy-start
  0.0 8.1 %collective-permute-start.1 = (bf16[1,256,8,256]{3,2,1,0:T(8,128)(2,1)}, bf16[1,256,8,256]{3,2,1,0:T(8,128)(2,1)S(1)}, u32[]{:S(2)}, u32[]{:S(2)}) collective-permute-start(bf16[1,256,8,256]{3,2,1,0:T(8,128)(2,1)} %param.8), channel_id=1, source_target_pairs={{8,0},{16,8},{24,16},{32,24},{40,32},{48,40},{56,48},{64,56},{72,6... | collective-permute-start | bytes 3145736 | tf_op jit(solution)/shard_map/ppermute | solution.py:18
  8.2 1.9 %collective-permute-start = (bf16[1,256,8,256]{3,2,1,0:T(8,128)(2,1)}, bf16[1,256,8,256]{3,2,1,0:T(8,128)(2,1)S(1)}, u32[]{:S(2)}, u32[]{:S(2)}) collective-permute-start(bf16[1,256,8,256]{3,2,1,0:T(8,128)(2,1)} %param.8), channel_id=1, source_target_pairs={{0,8},{8,16},{16,24},{24,32},{32,40},{40,48},{48,56},{56,64},{64,7... | collective-permute-start | bytes 3145736 | tf_op jit(solution)/shard_map/ppermute | solution.py:15
  10.1 1.7 %fusion.46 = f32[2048,256]{1,0:T(8,128)S(1)} fusion(bf16[1,256,8,256]{3,2,1,0:T(8,128)(2,1)} %param.8, bf16[3,3,256,256]{3,2,1,0:T(8,128)(2,1)} %param.9), kind=kOutput, calls=%fused_computation.61 | convolution fusion | flops 268435456 | bytes 3276800 | tf_op jit(solution)/shard_map/dot_general | solution.py:54
  11.8 0.0 copy-start.4
  11.8 19.1 %collective-permute-done.1 = bf16[1,256,8,256]{3,2,1,0:T(8,128)(2,1)S(1)} collective-permute-done((bf16[1,256,8,256]{3,2,1,0:T(8,128)(2,1)}, bf16[1,256,8,256]{3,2,1,0:T(8,128)(2,1)S(1)}, u32[]{:S(2)}, u32[]{:S(2)}) %collective-permute-start.1) | collective-permute-done | bytes 1048608 | tf_op jit(solution)/shard_map/ppermute | solution.py:18
  30.9 6.1 %collective-permute-done = bf16[1,256,8,256]{3,2,1,0:T(8,128)(2,1)S(1)} collective-permute-done((bf16[1,256,8,256]{3,2,1,0:T(8,128)(2,1)}, bf16[1,256,8,256]{3,2,1,0:T(8,128)(2,1)S(1)}, u32[]{:S(2)}, u32[]{:S(2)}) %collective-permute-start) | collective-permute-done | bytes 1048608 | tf_op jit(solution)/shard_map/ppermute | solution.py:15
  37.0 0.0 copy-done.2
  37.0 0.6 fusion.11
  37.6 0.0 copy-done.4
  37.6 0.4 fusion.40
  38.0 0.4 fusion.41
  38.4 0.4 fusion.42
  38.9 0.4 fusion.43
  39.3 0.4 fusion.39
  39.8 0.4 fusion.48
  40.2 0.0 copy-start.8
  40.2 0.4 fusion.44
  40.6 0.2 copy-done.8
  40.9 1.7 %convert_reduce_fusion = (f32[2048]{0:T(1024)S(1)}, bf16[2048,256]{1,0:T(8,128)(2,1)S(1)}) fusion(f32[256]{0:T(256)S(1)} %copy-done.8, f32[2048,256]{1,0:T(8,128)S(1)} %fusion.39, f32[2048,256]{1,0:T(8,128)S(1)} %fusion.44, f32[2048,256]{1,0:T(8,128)S(1)} %fusion.40, bf16[3,3,256,256]{3,2,1,0:T(8,128)(2,1)S(1)} %copy-done.4, ...), kind=kOutput, calls=%fused_computation.17 | convolution fusion | flops 278919168 | bytes 19014656 | tf_op jit(solution)/shard_map/dot_general | solution.py:54
  42.6 0.6 fusion.19
  43.3 0.0 copy-done.9
  43.3 0.7 fusion.38
  44.0 20.4 %all_to_all.30 = bf16[1,256,8,256]{3,2,0,1:T(8,128)(2,1)S(1)} all-to-all(bf16[1,256,8,256]{3,2,0,1:T(8,128)(2,1)S(1)} %fusion.38), channel_id=1, replica_groups=mesh['lat'=32,'lead'=8] {'lead'}, dimensions={1} | all-to-all | bytes 2097152 | tf_op jit(solution)/shard_map/all_to_all | solution.py:61
  64.4 0.1 copy.33
  64.5 0.0 copy-done
  64.6 1.4 %convolution_convert_fusion = bf16[2048,256]{1,0:T(8,128)(2,1)} fusion(bf16[2048,256]{1,0:T(8,128)(2,1)S(1)} %bitcast.91, bf16[256,256]{1,0:T(8,128)(2,1)S(1)} %copy-done), kind=kOutput, calls=%fused_computation.25 | convolution fusion | flops 268959744 | bytes 2228224 | tf_op jit(solution)/shard_map/dot_general | solution.py:42
  66.0 1.5 %copy.36 = bf16[2048,256]{0,1:T(8,128)(2,1)S(1)} copy(bf16[2048,256]{1,0:T(8,128)(2,1)} %convolution_convert_fusion) | data formatting | bytes 2097152 | tf_op jit(solution)/shard_map/convert_element_type | solution.py:43
  67.4 0.0 copy-start.5
  67.5 0.0 copy-start.6
  67.5 3.2 %reshape_reshape.11 = bf16[32,64,8,32]{1,0,3,2:T(8,128)(2,1)} reshape(bf16[2048,256]{0,1:T(8,128)(2,1)S(1)} %copy.36) | data formatting | bytes 2097152 | tf_op jit(solution)/shard_map/reshape;reshape | solution.py:28
  70.7 0.0 copy-done.5
  70.7 0.4 convolution_convert_fusion.1
  71.1 0.0 copy-done.6
  71.1 1.4 %convolution_convert_fusion.2 = bf16[2048,256]{1,0:T(8,128)(2,1)} fusion(bf16[2048,256]{1,0:T(8,128)(2,1)S(1)} %bitcast.93, bf16[256,256]{1,0:T(8,128)(2,1)S(1)} %copy-done.6), kind=kOutput, calls=%fused_computation.27 | convolution fusion | flops 268959744 | bytes 2228224 | tf_op jit(solution)/shard_map/dot_general | solution.py:42
  72.5 2.3 %copy.34 = bf16[2048,256]{0,1:T(8,128)(2,1)} copy(bf16[2048,256]{1,0:T(8,128)(2,1)} %convolution_convert_fusion.2) | data formatting | bytes 2097152 | tf_op jit(solution)/shard_map/convert_element_type | solution.py:43
  74.8 0.6 copy.35
  75.4 3.2 %reshape_reshape.10 = bf16[32,64,8,32]{1,0,3,2:T(8,128)(2,1)} reshape(bf16[2048,256]{0,1:T(8,128)(2,1)S(1)} %copy.35) | data formatting | bytes 2097152 | tf_op jit(solution)/shard_map/reshape;reshape | solution.py:27
  78.6 4.6 %reshape_reshape.9 = bf16[32,64,8,32]{1,0,3,2:T(8,128)(2,1)} reshape(bf16[2048,256]{0,1:T(8,128)(2,1)} %copy.34) | data formatting | bytes 2097152 | tf_op jit(solution)/shard_map/reshape;reshape | solution.py:29
  83.2 4.4 %fusion.31 = f32[32,8,64,64]{2,3,1,0:T(8,128)S(1)} fusion(bf16[32,64,8,32]{1,0,3,2:T(8,128)(2,1)S(1)} %copy-done.1, bf16[32,64,8,32]{1,0,3,2:T(8,128)(2,1)} %reshape_reshape.10), kind=kOutput, calls=%fused_computation.42 | convolution fusion | flops 67108864 | bytes 6291456 | tf_op jit(solution)/shard_map/pqhd,pkhd->phqk/dot_general | solution.py:30
  87.5 12.2 %fusion.69 = (f32[32,8,64]{2,1,0:T(8,128)S(1)}, f32[32,8,64,64]{2,3,1,0:T(8,128)S(1)}) fusion(f32[32,8,64,64]{2,3,1,0:T(8,128)S(1)} %fusion.31), kind=kOutput, calls=%fused_computation.87 | output fusion | flops 4194367 | bytes 8454144 | tf_op jit(solution)/shard_map/sub | solution.py:34
  99.7 3.8 %fusion.34 = bf16[32,8,32,64]{3,2,1,0:T(8,128)(2,1)} fusion(f32[32,8,64,64]{2,3,1,0:T(8,128)S(1)} %get-tuple-element.8, f32[32,8,64]{2,1,0:T(8,128)S(1)} %get-tuple-element.7, bf16[32,64,8,32]{1,0,3,2:T(8,128)(2,1)S(1)} %copy-done.3), kind=kOutput, calls=%fused_computation.45 | convolution fusion | flops 69730304 | bytes 6356992 | tf_op jit(solution)/shard_map/phqk,pkhd->pqhd/dot_general | solution.py:36
  103.5 2.7 %copy.41 = bf16[1,32,64,256]{3,1,0,2:T(8,128)(2,1)S(1)} copy(bf16[1,32,64,256]{2,3,1,0:T(8,128)(2,1)} %bitcast.97) | data formatting | bytes 2097152 | tf_op jit(solution)/shard_map/reshape | solution.py:37
  106.2 18.5 %all_to_all.31 = bf16[1,32,64,256]{3,1,0,2:T(8,128)(2,1)S(1)} all-to-all(bf16[1,32,64,256]{3,1,0,2:T(8,128)(2,1)S(1)} %copy.41), channel_id=1, replica_groups=mesh['lat'=32,'lead'=8] {'lead'}, dimensions={2} | all-to-all | bytes 2097152 | tf_op jit(solution)/shard_map/all_to_all | solution.py:63
  124.7 0.6 copy.54
  125.3 0.1 copy.43
  125.4 0.2 copy-done.7
  125.6 1.4 %fusion.37 = bf16[1,256,8,256]{3,2,1,0:T(8,128)(2,1)} fusion(bf16[2048,256]{1,0:T(8,128)(2,1)S(1)} %bitcast.94, bf16[256,256]{1,0:T(8,128)(2,1)S(1)} %copy-done.7, bf16[2048,256]{1,0:T(8,128)(2,1)S(1)} %get-tuple-element.6), kind=kOutput, calls=%fused_computation.46 | convolution fusion | flops 270008320 | bytes 3276800 | tf_op jit(solution)/shard_map/dot_general | solution.py:64
  (9 shorter events, 0.0 us)
Async XLA Ops:
  0.0 64.5 %copy-start = (bf16[256,256]{1,0:T(8,128)(2,1)S(1)}, bf16[256,256]{1,0:T(8,128)(2,1)}, u32[]{:S(2)}) copy-start(bf16[256,256]{1,0:T(8,128)(2,1)} %param.13) | copy-start | bytes 393220
  0.0 37.0 %copy-start.2 = (bf16[1,256,8,256]{3,2,1,0:T(8,128)(2,1)S(1)}, bf16[1,256,8,256]{3,2,1,0:T(8,128)(2,1)}, u32[]{:S(2)}) copy-start(bf16[1,256,8,256]{3,2,1,0:T(8,128)(2,1)} %param.8) | copy-start | bytes 3145732
  0.0 30.9 %collective-permute-start.1 = (bf16[1,256,8,256]{3,2,1,0:T(8,128)(2,1)}, bf16[1,256,8,256]{3,2,1,0:T(8,128)(2,1)S(1)}, u32[]{:S(2)}, u32[]{:S(2)}) collective-permute-start(bf16[1,256,8,256]{3,2,1,0:T(8,128)(2,1)} %param.8), channel_id=1, source_target_pairs={{8,0},{16,8},{24,16},{32,24},{40,32},{48,40},{56,48},{64,56},{72,6... | collective-permute-start | bytes 3145736 | tf_op jit(solution)/shard_map/ppermute | solution.py:18
  8.2 28.8 %collective-permute-start = (bf16[1,256,8,256]{3,2,1,0:T(8,128)(2,1)}, bf16[1,256,8,256]{3,2,1,0:T(8,128)(2,1)S(1)}, u32[]{:S(2)}, u32[]{:S(2)}) collective-permute-start(bf16[1,256,8,256]{3,2,1,0:T(8,128)(2,1)} %param.8), channel_id=1, source_target_pairs={{0,8},{8,16},{16,24},{24,32},{32,40},{40,48},{48,56},{56,64},{64,7... | collective-permute-start | bytes 3145736 | tf_op jit(solution)/shard_map/ppermute | solution.py:15
  11.8 25.8 %copy-start.4 = (bf16[3,3,256,256]{3,2,1,0:T(8,128)(2,1)S(1)}, bf16[3,3,256,256]{3,2,1,0:T(8,128)(2,1)}, u32[]{:S(2)}) copy-start(bf16[3,3,256,256]{3,2,1,0:T(8,128)(2,1)} %param.9) | copy-start | bytes 3538948
  40.2 0.7 copy-start.8
  40.9 2.4 %copy-start.9 = (f32[256]{0:T(256)S(1)}, f32[256]{0:T(256)}, u32[]{:S(2)}) copy-start(f32[256]{0:T(256)} %param.11) | copy-start | bytes 3076
  67.4 3.2 %copy-start.5 = (bf16[256,256]{1,0:T(8,128)(2,1)S(1)}, bf16[256,256]{1,0:T(8,128)(2,1)}, u32[]{:S(2)}) copy-start(bf16[256,256]{1,0:T(8,128)(2,1)} %param.12) | copy-start | bytes 393220
  67.5 3.7 %copy-start.6 = (bf16[256,256]{1,0:T(8,128)(2,1)S(1)}, bf16[256,256]{1,0:T(8,128)(2,1)}, u32[]{:S(2)}) copy-start(bf16[256,256]{1,0:T(8,128)(2,1)} %param.14) | copy-start | bytes 393220
  78.6 4.6 %copy-start.1 = (bf16[32,64,8,32]{1,0,3,2:T(8,128)(2,1)S(1)}, bf16[32,64,8,32]{1,0,3,2:T(8,128)(2,1)}, u32[]{:S(2)}) copy-start(bf16[32,64,8,32]{1,0,3,2:T(8,128)(2,1)} %reshape_reshape.11) | copy-start | bytes 3145732
  87.5 12.2 %copy-start.3 = (bf16[32,64,8,32]{1,0,3,2:T(8,128)(2,1)S(1)}, bf16[32,64,8,32]{1,0,3,2:T(8,128)(2,1)}, u32[]{:S(2)}) copy-start(bf16[32,64,8,32]{1,0,3,2:T(8,128)(2,1)} %reshape_reshape.9) | copy-start | bytes 3145732
  124.7 0.9 copy-start.7
where the time goes:
time: 127 us
  blocking collectives  38.9 us (31%)
  waiting for transfers between devices  25.2 us (20%)
  local copies, waits for them, and re-layouts  19.3 us (15%)
  matrix products  19.2 us (15%)
  other arithmetic  14.1 us (11%)
  starting transfers between devices  10.1 us (8%)
    all_to_all x1, blocking collectives, shards(): lax.all_to_all(normed, 'lead', split_axis=1, concat_axis=2, tiled=True)  20.4 us
    ppermute x1, waiting for transfers between devices, padded_2(): lax.ppermute(lax.slice_in_dim(block, 0, width, axis=dim), axis, backward)  19.1 us
    all_to_all x1, blocking collectives, shards(): lax.all_to_all(attended_px, 'lead', split_axis=2, concat_axis=1, tiled=True)  18.5 us
    sub x1, other arithmetic, attend(): expo = jnp.exp(scores - top)  12.2 us
    ppermute x1, starting transfers between devices, padded_2(): lax.ppermute(lax.slice_in_dim(block, 0, width, axis=dim), axis, backward)  8.15 us
    dot_general x9, matrix products, shards(): jnp.dot(piece, conv_weight[a, b], preferred_element_type=jnp.float32)  6.44 us
    ppermute x1, waiting for transfers between devices, padded_2(): lax.ppermute(lax.slice_in_dim(block, block.shape[dim] - width, None, axis...  6.12 us
    another operation x1, local copies, waits for them, and re-layouts, attend(): values = values.reshape(-1, values.shape[-2], heads, HD)  4.55 us
  transfers between devices with their start and end apart: 2, of which 2 were waited for; matrix products, arithmetic and copies ran while one was open for 1% of the time, Pallas kernels for 0%

commit v1 on v0

--- a/solution.py
+++ b/solution.py
@@ -58,7 +58,19 @@
     var = jnp.mean((hidden_f - mean) ** 2, axis=-1, keepdims=True)
     normed = ((hidden_f - mean) * lax.rsqrt(var + 1e-05) * norm_gain).astype(jnp.bfloat16)
     normed = normed.reshape(nrows, width, leads, chans)
-    block = lax.all_to_all(normed, "lead", split_axis=1, concat_axis=2, tiled=True)
+    ways, here = (lax.axis_size("lead"), lax.axis_index("lead"))
+    width_2 = normed.shape[1] // ways
+    lengths = list(normed.shape)
+    lengths[1] = width_2
+    height = lengths[2]
+    lengths[2] = height * ways
+    full = jnp.zeros(lengths, normed.dtype)
+    for mask in range(ways):
+        part = lax.dynamic_slice_in_dim(normed, (here ^ mask) * width_2, width_2, axis=1)
+        if mask:
+            part = lax.ppermute(part, "lead", [(d, d ^ mask) for d in range(ways)])
+        full = lax.dynamic_update_slice_in_dim(full, part, (here ^ mask) * height, axis=2)
+    block = full
     attended_px = attend(project(block, w_query), project(block, w_key), project(block, w_value))
     attended = lax.all_to_all(attended_px, "lead", split_axis=2, concat_axis=1, tiled=True)
     mixed = hidden_f + jnp.dot(

time: 127 us -> 119 us (0.937)
  blocking collectives: 38.9 us -> 19.5 us
  starting transfers between devices: 10.1 us -> 18.4 us
  waiting for transfers between devices: 25.2 us -> 32.9 us
  other arithmetic: 14.1 us -> 6.44 us
  matrix products: 19.2 us -> 23.9 us
  local copies, waits for them, and re-layouts: 19.3 us -> 17.3 us
    all_to_all x1 -> x0, blocking collectives: 20.4 us -> none  [shards(): lax.all_to_all(normed, 'lead', split_axis=1, concat_axis=2, tiled=True)]
    ppermute x1, waiting for transfers between devices: 19.1 us -> 1.29 us  [padded_2(): lax.ppermute(lax.slice_in_dim(block, 0, width, axis=dim), axis, backward)]
    ppermute x1, waiting for transfers between devices: 6.12 us -> 19.7 us  [padded_2(): lax.ppermute(lax.slice_in_dim(block, block.shape[dim] - width, None, axis...]
    ppermute x0 -> x7, waiting for transfers between devices: none -> 11.9 us  [shards(): part = lax.ppermute(part, 'lead', [(d, d ^ mask) for d in range(ways)])]
    ppermute x0 -> x7, starting transfers between devices: none -> 8.33 us  [shards(): part = lax.ppermute(part, 'lead', [(d, d ^ mask) for d in range(ways)])]
    sub x1, other arithmetic: 12.2 us -> 4.5 us  [attend(): expo = jnp.exp(scores - top)]
    dot_general x1, matrix products: 3.8 us -> 7.81 us  [attend(): jnp.einsum('phqk,pkhd->pqhd', weights, values, preferred_element_type=jnp...]
    ppermute x1, starting transfers between devices: 8.15 us -> 6.12 us  [padded_2(): lax.ppermute(lax.slice_in_dim(block, 0, width, axis=dim), axis, backward)]
  transfers between devices with their start and end apart: 2 -> 9, of which waited for: 2 -> 6; matrix products, arithmetic and copies ran while one was open for 1% -> 1% of each run, Pallas kernels for 0% -> 0%
where the time goes in v1:
time: 119 us
  waiting for transfers between devices  32.9 us (28%)
  matrix products  23.9 us (20%)
  blocking collectives  19.5 us (16%)
  starting transfers between devices  18.4 us (15%)
  local copies, waits for them, and re-layouts  17.3 us (15%)
  other arithmetic  6.44 us (5%)
    ppermute x1, waiting for transfers between devices, padded_2(): lax.ppermute(lax.slice_in_dim(block, block.shape[dim] - width, None, axis...  19.7 us
    all_to_all x1, blocking collectives, shards(): lax.all_to_all(attended_px, 'lead', split_axis=2, concat_axis=1, tiled=True)  19.5 us
    ppermute x7, waiting for transfers between devices, shards(): part = lax.ppermute(part, 'lead', [(d, d ^ mask) for d in range(ways)])  11.9 us
    ppermute x7, starting transfers between devices, shards(): part = lax.ppermute(part, 'lead', [(d, d ^ mask) for d in range(ways)])  8.33 us
    dot_general x1, matrix products, attend(): jnp.einsum('phqk,pkhd->pqhd', weights, values, preferred_element_type=jnp...  7.81 us
    dot_general x9, matrix products, shards(): jnp.dot(piece, conv_weight[a, b], preferred_element_type=jnp.float32)  6.44 us
    ppermute x1, starting transfers between devices, padded_2(): lax.ppermute(lax.slice_in_dim(block, 0, width, axis=dim), axis, backward)  6.12 us
    dot_general x1, matrix products, attend(): jnp.einsum('pqhd,pkhd->phqk', query, keys, preferred_element_type=jnp.flo...  5.02 us
  transfers between devices with their start and end apart: 9, of which 6 were waited for; matrix products, arithmetic and copies ran while one was open for 1% of the time, Pallas kernels for 0%

profile of v1, /device:TPU:6, one launch (start us, length us, event | category | flops | bytes accessed | tf_op | source)
XLA Modules:
  0.0 118.7 jit_solution(8214232237816704027)
XLA Ops:
  0.0 3.9 %collective-permute-start = (bf16[1,256,8,256]{3,2,1,0:T(8,128)(2,1)}, bf16[1,256,8,256]{3,2,1,0:T(8,128)(2,1)S(1)}, u32[]{:S(2)}, u32[]{:S(2)}) collective-permute-start(bf16[1,256,8,256]{3,2,1,0:T(8,128)(2,1)} %param.8), channel_id=1, source_target_pairs={{0,8},{8,16},{16,24},{24,32},{32,40},{40,48},{48,56},{56,64},{64,7... | collective-permute-start | bytes 3145736 | tf_op jit(solution)/shard_map/ppermute | solution.py:15
  4.0 6.1 %collective-permute-start.1 = (bf16[1,256,8,256]{3,2,1,0:T(8,128)(2,1)}, bf16[1,256,8,256]{3,2,1,0:T(8,128)(2,1)S(1)}, u32[]{:S(2)}, u32[]{:S(2)}) collective-permute-start(bf16[1,256,8,256]{3,2,1,0:T(8,128)(2,1)} %param.8), channel_id=1, source_target_pairs={{8,0},{16,8},{24,16},{32,24},{40,32},{48,40},{56,48},{64,56},{72,6... | collective-permute-start | bytes 3145736 | tf_op jit(solution)/shard_map/ppermute | solution.py:18
  10.1 1.7 %fusion.46 = f32[2048,256]{1,0:T(8,128)S(1)} fusion(bf16[1,256,8,256]{3,2,1,0:T(8,128)(2,1)} %param.8, bf16[3,3,256,256]{3,2,1,0:T(8,128)(2,1)} %param.9), kind=kOutput, calls=%fused_computation.61 | convolution fusion | flops 268435456 | bytes 3276800 | tf_op jit(solution)/shard_map/dot_general | solution.py:54
  11.8 19.7 %collective-permute-done = bf16[1,256,8,256]{3,2,1,0:T(8,128)(2,1)S(1)} collective-permute-done((bf16[1,256,8,256]{3,2,1,0:T(8,128)(2,1)}, bf16[1,256,8,256]{3,2,1,0:T(8,128)(2,1)S(1)}, u32[]{:S(2)}, u32[]{:S(2)}) %collective-permute-start) | collective-permute-done | bytes 1048608 | tf_op jit(solution)/shard_map/ppermute | solution.py:15
  31.5 1.3 %collective-permute-done.1 = bf16[1,256,8,256]{3,2,1,0:T(8,128)(2,1)S(1)} collective-permute-done((bf16[1,256,8,256]{3,2,1,0:T(8,128)(2,1)}, bf16[1,256,8,256]{3,2,1,0:T(8,128)(2,1)S(1)}, u32[]{:S(2)}, u32[]{:S(2)}) %collective-permute-start.1) | collective-permute-done | bytes 1048608 | tf_op jit(solution)/shard_map/ppermute | solution.py:18
  32.8 0.6 fusion.11
  33.4 0.4 fusion.39
  33.8 0.4 fusion.40
  34.3 0.4 fusion.41
  34.7 0.4 fusion.42
  35.1 0.4 fusion.43
  35.6 0.4 fusion.44
  36.0 0.4 fusion.48
  36.5 0.2 copy-done.6
  36.7 1.7 %convert_reduce_fusion = (f32[2048]{0:T(1024)S(1)}, bf16[2048,256]{1,0:T(8,128)(2,1)S(1)}) fusion(f32[256]{0:T(256)S(1)} %copy-done.6, f32[2048,256]{1,0:T(8,128)S(1)} %fusion.39, f32[2048,256]{1,0:T(8,128)S(1)} %fusion.44, f32[2048,256]{1,0:T(8,128)S(1)} %fusion.40, bf16[3,3,256,256]{3,2,1,0:T(8,128)(2,1)S(1)} %copy-done.2, ...), kind=kOutput, calls=%fused_computation.17 | convolution fusion | flops 278919168 | bytes 19014656 | tf_op jit(solution)/shard_map/dot_general | solution.py:54
  38.5 0.6 fusion.19
  39.1 0.7 fusion.38
  39.9 0.1 broadcast_in_dim.2
  40.0 0.1 constant_dynamic-slice_fusion
  40.1 0.1 collective-permute-start.2
  40.2 1.7 %collective-permute-start.3 = (bf16[1,32,8,256]{3,2,1,0:T(8,128)(2,1)S(1)}, bf16[1,32,8,256]{3,2,1,0:T(8,128)(2,1)S(1)}, u32[]{:S(2)}, u32[]{:S(2)}) collective-permute-start(bf16[1,32,8,256]{3,2,1,0:T(8,128)(2,1)S(1)} %get-tuple-element.10), channel_id=1, source_target_pairs={{0,2},{1,3},{2,0},{3,1},{4,6},{5,7},{6,4},{7,5},{8,10},{9,11},{10,... | collective-permute-start | bytes 393224 | tf_op jit(solution)/shard_map/ppermute | solution.py:71
  41.8 0.2 collective-permute-start.4
  42.0 3.2 %collective-permute-start.5 = (bf16[1,32,8,256]{3,2,1,0:T(8,128)(2,1)S(1)}, bf16[1,32,8,256]{3,2,1,0:T(8,128)(2,1)S(1)}, u32[]{:S(2)}, u32[]{:S(2)}) collective-permute-start(bf16[1,32,8,256]{3,2,1,0:T(8,128)(2,1)S(1)} %get-tuple-element.8), channel_id=1, source_target_pairs={{0,4},{1,5},{2,6},{3,7},{4,0},{5,1},{6,2},{7,3},{8,12},{9,13},{10,... | collective-permute-start | bytes 393224 | tf_op jit(solution)/shard_map/ppermute | solution.py:71
  45.3 0.0 collective-permute-start.6
  45.3 3.0 %collective-permute-start.7 = (bf16[1,32,8,256]{3,2,1,0:T(8,128)(2,1)S(1)}, bf16[1,32,8,256]{3,2,1,0:T(8,128)(2,1)S(1)}, u32[]{:S(2)}, u32[]{:S(2)}) collective-permute-start(bf16[1,32,8,256]{3,2,1,0:T(8,128)(2,1)S(1)} %get-tuple-element.6), channel_id=1, source_target_pairs={{0,6},{1,7},{2,4},{3,5},{4,2},{5,3},{6,0},{7,1},{8,14},{9,15},{10,... | collective-permute-start | bytes 393224 | tf_op jit(solution)/shard_map/ppermute | solution.py:71
  48.3 0.1 collective-permute-start.8
  48.5 6.2 %collective-permute-done.5 = bf16[1,32,8,256]{3,2,1,0:T(8,128)(2,1)S(1)} collective-permute-done((bf16[1,32,8,256]{3,2,1,0:T(8,128)(2,1)S(1)}, bf16[1,32,8,256]{3,2,1,0:T(8,128)(2,1)S(1)}, u32[]{:S(2)}, u32[]{:S(2)}) %collective-permute-start.5) | collective-permute-done | bytes 131104 | tf_op jit(solution)/shard_map/ppermute | solution.py:71
  54.8 1.8 %collective-permute-done.6 = bf16[1,32,8,256]{3,2,1,0:T(8,128)(2,1)S(1)} collective-permute-done((bf16[1,32,8,256]{3,2,1,0:T(8,128)(2,1)S(1)}, bf16[1,32,8,256]{3,2,1,0:T(8,128)(2,1)S(1)}, u32[]{:S(2)}, u32[]{:S(2)}) %collective-permute-start.6) | collective-permute-done | bytes 131104 | tf_op jit(solution)/shard_map/ppermute | solution.py:71
  56.6 1.8 %collective-permute-done.7 = bf16[1,32,8,256]{3,2,1,0:T(8,128)(2,1)S(1)} collective-permute-done((bf16[1,32,8,256]{3,2,1,0:T(8,128)(2,1)S(1)}, bf16[1,32,8,256]{3,2,1,0:T(8,128)(2,1)S(1)}, u32[]{:S(2)}, u32[]{:S(2)}) %collective-permute-start.7) | collective-permute-done | bytes 131104 | tf_op jit(solution)/shard_map/ppermute | solution.py:71
  58.4 2.0 %collective-permute-done.8 = bf16[1,32,8,256]{3,2,1,0:T(8,128)(2,1)S(1)} collective-permute-done((bf16[1,32,8,256]{3,2,1,0:T(8,128)(2,1)S(1)}, bf16[1,32,8,256]{3,2,1,0:T(8,128)(2,1)S(1)}, u32[]{:S(2)}, u32[]{:S(2)}) %collective-permute-start.8) | collective-permute-done | bytes 131104 | tf_op jit(solution)/shard_map/ppermute | solution.py:71
  60.4 1.4 %convolution_convert_fusion.1 = bf16[2048,256]{1,0:T(8,128)(2,1)} fusion(bf16[2048,256]{1,0:T(8,128)(2,1)S(1)} %bitcast.86, bf16[256,256]{1,0:T(8,128)(2,1)S(1)} %copy-done), kind=kOutput, calls=%fused_computation.26 | convolution fusion | flops 268959744 | bytes 2228224 | tf_op jit(solution)/shard_map/dot_general | solution.py:42
  61.8 1.5 %copy.23 = bf16[2048,256]{0,1:T(8,128)(2,1)S(1)} copy(bf16[2048,256]{1,0:T(8,128)(2,1)} %convolution_convert_fusion.1) | data formatting | bytes 2097152 | tf_op jit(solution)/shard_map/convert_element_type | solution.py:43
  63.3 3.2 %reshape_reshape.10 = bf16[32,64,8,32]{1,0,3,2:T(8,128)(2,1)} reshape(bf16[2048,256]{0,1:T(8,128)(2,1)S(1)} %copy.23) | data formatting | bytes 2097152 | tf_op jit(solution)/shard_map/reshape;reshape | solution.py:27
  66.5 1.4 %convolution_convert_fusion = bf16[2048,256]{1,0:T(8,128)(2,1)} fusion(bf16[2048,256]{1,0:T(8,128)(2,1)S(1)} %bitcast.87, bf16[256,256]{1,0:T(8,128)(2,1)S(1)} %copy-done.3), kind=kOutput, calls=%fused_computation.25 | convolution fusion | flops 268959744 | bytes 2228224 | tf_op jit(solution)/shard_map/dot_general | solution.py:42
  67.9 1.5 %copy.24 = bf16[2048,256]{0,1:T(8,128)(2,1)S(1)} copy(bf16[2048,256]{1,0:T(8,128)(2,1)} %convolution_convert_fusion) | data formatting | bytes 2097152 | tf_op jit(solution)/shard_map/convert_element_type | solution.py:43
  69.4 3.2 %reshape_reshape.11 = bf16[32,64,8,32]{1,0,3,2:T(8,128)(2,1)} reshape(bf16[2048,256]{0,1:T(8,128)(2,1)S(1)} %copy.24) | data formatting | bytes 2097152 | tf_op jit(solution)/shard_map/reshape;reshape | solution.py:28
  72.6 5.0 %fusion.31 = f32[32,8,64,64]{2,3,1,0:T(8,128)S(1)} fusion(bf16[32,64,8,32]{1,0,3,2:T(8,128)(2,1)} %reshape_reshape.11, bf16[32,64,8,32]{1,0,3,2:T(8,128)(2,1)} %reshape_reshape.10), kind=kOutput, calls=%fused_computation.42 | convolution fusion | flops 67108864 | bytes 6291456 | tf_op jit(solution)/shard_map/pqhd,pkhd->phqk/dot_general | solution.py:30
  77.7 4.5 %fusion.69 = (f32[32,8,64]{2,1,0:T(8,128)S(1)}, f32[32,8,64,64]{2,3,1,0:T(8,128)}) fusion(f32[32,8,64,64]{2,3,1,0:T(8,128)S(1)} %fusion.31), kind=kOutput, calls=%fused_computation.102 | output fusion | flops 4194367 | bytes 8454144 | tf_op jit(solution)/shard_map/sub | solution.py:34
  82.2 0.4 convolution_convert_fusion.2
  82.6 0.6 copy.22
  83.3 3.1 %reshape_reshape.9 = bf16[32,64,8,32]{1,0,3,2:T(8,128)(2,1)} reshape(bf16[2048,256]{0,1:T(8,128)(2,1)S(1)} %copy.22) | data formatting | bytes 2097152 | tf_op jit(solution)/shard_map/reshape;reshape | solution.py:29
  86.4 7.8 %fusion.34 = bf16[32,8,32,64]{3,2,1,0:T(8,128)(2,1)} fusion(f32[32,8,64,64]{2,3,1,0:T(8,128)} %get-tuple-element.16, f32[32,8,64]{2,1,0:T(8,128)S(1)} %get-tuple-element.15, bf16[32,64,8,32]{1,0,3,2:T(8,128)(2,1)} %reshape_reshape.9), kind=kOutput, calls=%fused_computation.45 | convolution fusion | flops 69730304 | bytes 6356992 | tf_op jit(solution)/shard_map/phqk,pkhd->pqhd/dot_general | solution.py:36
  94.2 2.7 %copy.29 = bf16[1,32,64,256]{3,1,0,2:T(8,128)(2,1)S(1)} copy(bf16[1,32,64,256]{2,3,1,0:T(8,128)(2,1)} %bitcast.91) | data formatting | bytes 2097152 | tf_op jit(solution)/shard_map/reshape | solution.py:37
  96.9 19.5 %all_to_all.15 = bf16[1,32,64,256]{3,1,0,2:T(8,128)(2,1)S(1)} all-to-all(bf16[1,32,64,256]{3,1,0,2:T(8,128)(2,1)S(1)} %copy.29), channel_id=1, replica_groups=mesh['lat'=32,'lead'=8] {'lead'}, dimensions={2} | all-to-all | bytes 2097152 | tf_op jit(solution)/shard_map/all_to_all | solution.py:75
  116.4 0.6 copy.42
  117.0 0.1 copy.31
  117.1 0.2 copy-done.5
  117.3 1.4 %fusion.37 = bf16[1,256,8,256]{3,2,1,0:T(8,128)(2,1)} fusion(bf16[2048,256]{1,0:T(8,128)(2,1)S(1)} %bitcast.89, bf16[256,256]{1,0:T(8,128)(2,1)S(1)} %copy-done.5, bf16[2048,256]{1,0:T(8,128)(2,1)S(1)} %get-tuple-element.14), kind=kOutput, calls=%fused_computation.46 | convolution fusion | flops 270008320 | bytes 3276800 | tf_op jit(solution)/shard_map/dot_general | solution.py:76
  (26 shorter events, 0.2 us)
Async XLA Ops:
  0.0 60.4 %copy-start = (bf16[256,256]{1,0:T(8,128)(2,1)S(1)}, bf16[256,256]{1,0:T(8,128)(2,1)}, u32[]{:S(2)}) copy-start(bf16[256,256]{1,0:T(8,128)(2,1)} %param.12) | copy-start | bytes 393220
  0.0 32.8 %copy-start.1 = (bf16[1,256,8,256]{3,2,1,0:T(8,128)(2,1)S(1)}, bf16[1,256,8,256]{3,2,1,0:T(8,128)(2,1)}, u32[]{:S(2)}) copy-start(bf16[1,256,8,256]{3,2,1,0:T(8,128)(2,1)} %param.8) | copy-start | bytes 3145732
  0.0 31.5 %collective-permute-start = (bf16[1,256,8,256]{3,2,1,0:T(8,128)(2,1)}, bf16[1,256,8,256]{3,2,1,0:T(8,128)(2,1)S(1)}, u32[]{:S(2)}, u32[]{:S(2)}) collective-permute-start(bf16[1,256,8,256]{3,2,1,0:T(8,128)(2,1)} %param.8), channel_id=1, source_target_pairs={{0,8},{8,16},{16,24},{24,32},{32,40},{40,48},{48,56},{56,64},{64,7... | collective-permute-start | bytes 3145736 | tf_op jit(solution)/shard_map/ppermute | solution.py:15
  4.0 28.8 %collective-permute-start.1 = (bf16[1,256,8,256]{3,2,1,0:T(8,128)(2,1)}, bf16[1,256,8,256]{3,2,1,0:T(8,128)(2,1)S(1)}, u32[]{:S(2)}, u32[]{:S(2)}) collective-permute-start(bf16[1,256,8,256]{3,2,1,0:T(8,128)(2,1)} %param.8), channel_id=1, source_target_pairs={{8,0},{16,8},{24,16},{32,24},{40,32},{48,40},{56,48},{64,56},{72,6... | collective-permute-start | bytes 3145736 | tf_op jit(solution)/shard_map/ppermute | solution.py:18
  11.8 21.6 %copy-start.2 = (bf16[3,3,256,256]{3,2,1,0:T(8,128)(2,1)S(1)}, bf16[3,3,256,256]{3,2,1,0:T(8,128)(2,1)}, u32[]{:S(2)}) copy-start(bf16[3,3,256,256]{3,2,1,0:T(8,128)(2,1)} %param.9) | copy-start | bytes 3538948
  36.0 0.7 copy-start.6
  36.7 2.4 %copy-start.7 = (f32[256]{0:T(256)S(1)}, f32[256]{0:T(256)}, u32[]{:S(2)}) copy-start(f32[256]{0:T(256)} %param.11) | copy-start | bytes 3076
  40.1 5.2 %collective-permute-start.2 = (bf16[1,32,8,256]{3,2,1,0:T(8,128)(2,1)S(1)}, bf16[1,32,8,256]{3,2,1,0:T(8,128)(2,1)S(1)}, u32[]{:S(2)}, u32[]{:S(2)}) collective-permute-start(bf16[1,32,8,256]{3,2,1,0:T(8,128)(2,1)S(1)} %get-tuple-element.11), channel_id=1, source_target_pairs={{0,1},{1,0},{2,3},{3,2},{4,5},{5,4},{6,7},{7,6},{8,9},{9,8},{10,11... | collective-permute-start | bytes 393224 | tf_op jit(solution)/shard_map/ppermute | solution.py:71
  40.2 8.1 %collective-permute-start.3 = (bf16[1,32,8,256]{3,2,1,0:T(8,128)(2,1)S(1)}, bf16[1,32,8,256]{3,2,1,0:T(8,128)(2,1)S(1)}, u32[]{:S(2)}, u32[]{:S(2)}) collective-permute-start(bf16[1,32,8,256]{3,2,1,0:T(8,128)(2,1)S(1)} %get-tuple-element.10), channel_id=1, source_target_pairs={{0,2},{1,3},{2,0},{3,1},{4,6},{5,7},{6,4},{7,5},{8,10},{9,11},{10,... | collective-permute-start | bytes 393224 | tf_op jit(solution)/shard_map/ppermute | solution.py:71
  41.8 6.6 %collective-permute-start.4 = (bf16[1,32,8,256]{3,2,1,0:T(8,128)(2,1)S(1)}, bf16[1,32,8,256]{3,2,1,0:T(8,128)(2,1)S(1)}, u32[]{:S(2)}, u32[]{:S(2)}) collective-permute-start(bf16[1,32,8,256]{3,2,1,0:T(8,128)(2,1)S(1)} %get-tuple-element.9), channel_id=1, source_target_pairs={{0,3},{1,2},{2,1},{3,0},{4,7},{5,6},{6,5},{7,4},{8,11},{9,10},{10,... | collective-permute-start | bytes 393224 | tf_op jit(solution)/shard_map/ppermute | solution.py:71
  42.0 12.7 %collective-permute-start.5 = (bf16[1,32,8,256]{3,2,1,0:T(8,128)(2,1)S(1)}, bf16[1,32,8,256]{3,2,1,0:T(8,128)(2,1)S(1)}, u32[]{:S(2)}, u32[]{:S(2)}) collective-permute-start(bf16[1,32,8,256]{3,2,1,0:T(8,128)(2,1)S(1)} %get-tuple-element.8), channel_id=1, source_target_pairs={{0,4},{1,5},{2,6},{3,7},{4,0},{5,1},{6,2},{7,3},{8,12},{9,13},{10,... | collective-permute-start | bytes 393224 | tf_op jit(solution)/shard_map/ppermute | solution.py:71
  45.3 11.3 %collective-permute-start.6 = (bf16[1,32,8,256]{3,2,1,0:T(8,128)(2,1)S(1)}, bf16[1,32,8,256]{3,2,1,0:T(8,128)(2,1)S(1)}, u32[]{:S(2)}, u32[]{:S(2)}) collective-permute-start(bf16[1,32,8,256]{3,2,1,0:T(8,128)(2,1)S(1)} %get-tuple-element.7), channel_id=1, source_target_pairs={{0,5},{1,4},{2,7},{3,6},{4,1},{5,0},{6,3},{7,2},{8,13},{9,12},{10,... | collective-permute-start | bytes 393224 | tf_op jit(solution)/shard_map/ppermute | solution.py:71
  45.3 13.1 %collective-permute-start.7 = (bf16[1,32,8,256]{3,2,1,0:T(8,128)(2,1)S(1)}, bf16[1,32,8,256]{3,2,1,0:T(8,128)(2,1)S(1)}, u32[]{:S(2)}, u32[]{:S(2)}) collective-permute-start(bf16[1,32,8,256]{3,2,1,0:T(8,128)(2,1)S(1)} %get-tuple-element.6), channel_id=1, source_target_pairs={{0,6},{1,7},{2,4},{3,5},{4,2},{5,3},{6,0},{7,1},{8,14},{9,15},{10,... | collective-permute-start | bytes 393224 | tf_op jit(solution)/shard_map/ppermute | solution.py:71
  48.3 12.1 %collective-permute-start.8 = (bf16[1,32,8,256]{3,2,1,0:T(8,128)(2,1)S(1)}, bf16[1,32,8,256]{3,2,1,0:T(8,128)(2,1)S(1)}, u32[]{:S(2)}, u32[]{:S(2)}) collective-permute-start(bf16[1,32,8,256]{3,2,1,0:T(8,128)(2,1)S(1)} %get-tuple-element.5), channel_id=1, source_target_pairs={{0,7},{1,6},{2,5},{3,4},{4,3},{5,2},{6,1},{7,0},{8,15},{9,14},{10,... | collective-permute-start | bytes 393224 | tf_op jit(solution)/shard_map/ppermute | solution.py:71
  63.3 3.2 %copy-start.3 = (bf16[256,256]{1,0:T(8,128)(2,1)S(1)}, bf16[256,256]{1,0:T(8,128)(2,1)}, u32[]{:S(2)}) copy-start(bf16[256,256]{1,0:T(8,128)(2,1)} %param.13) | copy-start | bytes 393220
  77.6 4.5 %copy-start.4 = (bf16[256,256]{1,0:T(8,128)(2,1)S(1)}, bf16[256,256]{1,0:T(8,128)(2,1)}, u32[]{:S(2)}) copy-start(bf16[256,256]{1,0:T(8,128)(2,1)} %param.14) | copy-start | bytes 393220
  116.4 0.9 copy-start.5
